TPU v7x, 256 devices: a whole 4x4x8 slice. The times are simulated.
256 devices in a mesh: row: 4 (over z_lo, core), col: 64 (over y, z_hi, x).
Axes of the slice: x: 4, y: 4, z: 8 (z_hi: 4, z_lo: 2; z = z_hi * 2 + z_lo), core: 2. Of those that a mesh axis runs over, the one named last changes fastest.
Arguments:
- tokens: bfloat16 [1024, 8192], P('col', 'row'), may hold values from -6 to 6
- out_grad: bfloat16 [1024, 8192], P('col', 'row'), may hold values from -2 to 2
- gate_weight: bfloat16 [8192, 28672], P('row', 'col'), may hold values from -0.0625 to 0.0625
- up_weight: bfloat16 [8192, 28672], P('row', 'col'), may hold values from -0.0625 to 0.0625
- down_weight: bfloat16 [28672, 8192], P('col', 'row'), may hold values from -0.03125 to 0.03125
Outputs:
- grad_input: bfloat16 [1024, 8192], P('col', 'row')
- grad_gate: bfloat16 [8192, 28672], P('row', 'col')
- grad_up: bfloat16 [8192, 28672], P('row', 'col')
- grad_down: bfloat16 [28672, 8192], P('col', 'row')
All inputs are finite; a program needn't handle non-finite values.
Results may differ from a plain program's by a relative error of at most 0.005.
Values may be sent and summed in bfloat16 or wider, within the bound.
No kernel may reach another device: no remote copies, remote signals or barrier semaphores. Data moves between devices by JAX's collectives and lax.ppermute only.
A program may use at most 128 MiB of HBM per device.

v0:
```python
import jax
import jax.numpy as jnp
from jax import lax
from jax.sharding import PartitionSpec as P


def pointwise(gate, up, hidden_grad):
    logistic = jax.nn.sigmoid(gate)
    active = gate * logistic
    hidden = (active * up).astype(jnp.bfloat16)
    d_gate = (hidden_grad * up * logistic * (1.0 + gate * (1.0 - logistic))).astype(jnp.bfloat16)
    d_up = (hidden_grad * active).astype(jnp.bfloat16)
    return (hidden, d_gate, d_up)


def contract_last(left, right):
    return lax.dot_general(
        left, right, (((1,), (1,)), ((), ())), preferred_element_type=jnp.float32
    )


def contract_first(left, right):
    return lax.dot_general(
        left, right, (((0,), (0,)), ((), ())), preferred_element_type=jnp.float32
    )


def local(tokens, out_grad, gate_weight, up_weight, down_weight):
    full_tokens, full_grad = (
        lax.all_gather(tokens, "col", axis=0, tiled=True),
        lax.all_gather(out_grad, "col", axis=0, tiled=True),
    )
    gate_part = jnp.dot(full_tokens, gate_weight, preferred_element_type=jnp.float32)
    up_part = jnp.dot(full_tokens, up_weight, preferred_element_type=jnp.float32)
    hidden_part = contract_last(full_grad, down_weight)
    gate, up, hidden_grad = lax.psum((gate_part, up_part, hidden_part), "row")
    hidden, d_gate, d_up = pointwise(gate, up, hidden_grad)
    grad_down = contract_first(hidden, full_grad).astype(jnp.bfloat16)
    grad_gate = contract_first(full_tokens, d_gate).astype(jnp.bfloat16)
    grad_up = contract_first(full_tokens, d_up).astype(jnp.bfloat16)
    grad_input = lax.psum_scatter(
        contract_last(d_gate, gate_weight) + contract_last(d_up, up_weight),
        "col",
        scatter_dimension=0,
        tiled=True,
    ).astype(jnp.bfloat16)
    return (grad_input, grad_gate, grad_up, grad_down)


def solution(mesh):
    in_specs = (P("col", "row"), P("col", "row"), P("row", "col"), P("row", "col"), P("col", "row"))
    out_specs = (P("col", "row"), P("row", "col"), P("row", "col"), P("col", "row"))
    return jax.shard_map(local, mesh=mesh, in_specs=in_specs, out_specs=out_specs, check_vma=False)
```

profile of v0, /device:TPU:0, one launch (start us, length us, event | category | flops | bytes accessed | tf_op | source)
XLA Modules:
  0.0 743.4 jit_solution(6476649636383026013)
XLA Ops:
  7.2 0.0 copy-start
  7.2 0.0 all-gather.5.cloned.1.call-start
  7.2 0.7 all-gather.5.cloned.1.call-update
  7.9 0.0 all-gather.3.cloned.1.call-start
  8.0 0.7 all-gather.3.cloned.1.call-update
  8.7 0.0 all-reduce.3.cloned.1.call-start
  8.7 93.1 %all-gather.5.cloned.1.call-done = bf16[1024,2048]{1,0:T(8,128)(2,1)} async-done(((bf16[16,2048]{1,0:T(8,128)(2,1)}), bf16[1024,2048]{1,0:T(8,128)(2,1)}) %all-gather.5.cloned.1.call-update) | async-done | bytes 4194320 | tf_op jit(solution)/shard_map/all_gather | solution.py:30
  101.8 5.7 fusion.7
  107.4 3.3 fusion.6
  110.8 82.0 %all-gather.3.cloned.1.call-done = bf16[1024,2048]{1,0:T(8,128)(2,1)} async-done(((bf16[16,2048]{1,0:T(8,128)(2,1)}), bf16[1024,2048]{1,0:T(8,128)(2,1)}) %all-gather.3.cloned.1.call-update) | async-done | bytes 4194320 | tf_op jit(solution)/shard_map/all_gather | solution.py:31
  192.7 6.1 fusion.5
  198.8 0.0 all-reduce.3.cloned.1.call-update
  198.9 0.2 reduce-scatter.2.cloned.1.call-start
  199.1 116.1 %all-reduce.3.cloned.1.call-done = (f32[1024,448]{0,1:T(8,128)}, f32[1024,448]{0,1:T(8,128)}, f32[1024,448]{0,1:T(8,128)}) async-done(((f32[1024,448]{0,1:T(8,128)}, f32[1024,448]{0,1:T(8,128)}, f32[1024,448]{0,1:T(8,128)}), (f32[1024,448]{0,1:T(8,128)}, f32[1024,448]{0,1:T(8,128)}, f32[1024,448]{0,1:T(8,128)})) %all-reduce.3.cloned.1.call-update) | async-done | bytes 5505040 | tf_op jit(solution)/shard_map/psum | solution.py:36
  315.2 3.7 multiply_convert_fusion.1
  318.9 2.4 fusion.8
  321.4 5.9 convolution_add_fusion
  327.3 0.0 reduce-scatter.2.cloned.1.call-update
  327.3 5.6 fusion.1
  333.0 3.3 fusion
  336.3 0.3 copy-done.9
  336.6 3.4 convolution_convert_fusion
  340.0 395.3 %reduce-scatter.2.cloned.1.call-done = f32[16,2048]{1,0:T(8,128)} async-done(((f32[1024,2048]{1,0:T(8,128)}), f32[16,2048]{1,0:T(8,128)}) %reduce-scatter.2.cloned.1.call-update) | async-done | bytes 131088 | tf_op jit(solution)/shard_map/reduce_scatter | solution.py:41
  735.3 1.5 convert_element_type.29
  (18 shorter events, 0.0 us)
Async XLA Ops:
  7.2 94.6 %copy-start = (bf16[2048,448]{0,1:T(8,128)(2,1)S(1)}, bf16[2048,448]{0,1:T(8,128)(2,1)}, u32[]{:S(2)}) copy-start(bf16[2048,448]{0,1:T(8,128)(2,1)} %param.7) | copy-start | bytes 5505028
  7.2 94.6 %all-gather.5.cloned.1.call-start = ((), (), s32[]{:S(2)}) async-start(), calls=%async_computation.2 | async-start | bytes 4259840 | tf_op jit(solution)/shard_map/all_gather | solution.py:30
  7.9 184.8 %all-gather.3.cloned.1.call-start = ((), (), s32[]{:S(2)}) async-start(), calls=%async_computation.1 | async-start | bytes 4259840 | tf_op jit(solution)/shard_map/all_gather | solution.py:31
  8.7 306.5 %all-reduce.3.cloned.1.call-start = ((), (), s32[]{:S(2)}) async-start(), calls=%async_computation.4 | async-start | bytes 11010048 | tf_op jit(solution)/shard_map/psum | solution.py:36
  101.8 5.7 copy-start.1
  101.8 5.7 copy-start.7
  198.9 536.4 %reduce-scatter.2.cloned.1.call-start = ((), (), s32[]{:S(2)}) async-start(), calls=%async_computation.3 | async-start | bytes 8519680 | tf_op jit(solution)/shard_map/reduce_scatter | solution.py:41
  318.9 2.4 copy-start.5
  318.9 2.4 copy-start.2
  327.3 5.7 copy-start.6
  327.3 5.7 copy-start.8
  332.9 3.4 copy-start.3
  332.9 3.4 copy-start.4
  333.0 3.7 copy-start.9
Sparse Core Ops, SparseCore 0:
  11.3 90.3 all-gather.4
  105.1 87.6 all-gather.2
  199.0 116.1 all-reduce.2
  327.4 407.8 reduce-scatter.1
where the time goes:
time: 743 us
  waiting for transfers between devices  688 us (93%)
  matrix products  35.7 us (5%)
  between operations  13.8 us (2%)
    reduce_scatter x1, waiting for transfers between devices, local(): lax.psum_scatter(contract_last(d_gate, gate_weight) + contract_last(d_up,...  395 us
    psum x1, waiting for transfers between devices, local(): gate, up, hidden_grad = lax.psum((gate_part, up_part, hidden_part), 'row')  116 us
    all_gather x1, waiting for transfers between devices, local(): lax.all_gather(tokens, 'col', axis=0, tiled=True)  93.1 us
    all_gather x1, waiting for transfers between devices, local(): lax.all_gather(out_grad, 'col', axis=0, tiled=True)  82 us
  transfers between devices with their start and end apart: 4, of which 4 were waited for; matrix products, arithmetic and copies ran while one was open for 3% of the time, Pallas kernels for 0%

commit v1 on v0

--- a/solution.py
+++ b/solution.py
@@ -28,7 +28,9 @@
 def local(tokens, out_grad, gate_weight, up_weight, down_weight):
     full_tokens, full_grad = (
         lax.all_gather(tokens, "col", axis=0, tiled=True),
-        lax.all_gather(out_grad, "col", axis=0, tiled=True),
+        jnp.concatenate(
+            lax.all_to_all(jnp.stack([out_grad] * lax.axis_size("col")), "col", 0, 0), axis=0
+        ),
     )
     gate_part = jnp.dot(full_tokens, gate_weight, preferred_element_type=jnp.float32)
     up_part = jnp.dot(full_tokens, up_weight, preferred_element_type=jnp.float32)

time: 743 us -> 701 us (0.943)
  waiting for transfers between devices: 688 us -> 627 us
  starting transfers between devices: 0.34 us -> 13.4 us
    all_to_all x0 -> x1, waiting for transfers between devices: none -> 110 us  [local(): lax.all_to_all(jnp.stack([out_grad] * lax.axis_size('col')), 'col', 0, 0)]
    all_gather x1, waiting for transfers between devices: 93.1 us -> 6.32 us  [local(): lax.all_gather(tokens, 'col', axis=0, tiled=True)]
    all_gather x1 -> x0, waiting for transfers between devices: 82 us -> none  [local(): lax.all_gather(out_grad, 'col', axis=0, tiled=True)]
    all_to_all x0 -> x1, starting transfers between devices: none -> 13.1 us  [local(): lax.all_to_all(jnp.stack([out_grad] * lax.axis_size('col')), 'col', 0, 0)]
where the time goes in v1:
time: 701 us
  waiting for transfers between devices  627 us (89%)
  matrix products  38 us (5%)
  between operations  13.8 us (2%)
  starting transfers between devices  13.4 us (2%)
    reduce_scatter x1, waiting for transfers between devices, local(): lax.psum_scatter(contract_last(d_gate, gate_weight) + contract_last(d_up,...  393 us
    psum x1, waiting for transfers between devices, local(): gate, up, hidden_grad = lax.psum((gate_part, up_part, hidden_part), 'row')  117 us
    all_to_all x1, waiting for transfers between devices, local(): lax.all_to_all(jnp.stack([out_grad] * lax.axis_size('col')), 'col', 0, 0)  110 us
    dot_general x3, matrix products, contract_first(): lax.dot_general(left, right, (((0,), (0,)), ((), ())), preferred_element_...  14.6 us
    dot_general x3, matrix products, contract_last(): lax.dot_general(left, right, (((1,), (1,)), ((), ())), preferred_element_...  14.5 us
  transfers between devices with their start and end apart: 4, of which 4 were waited for; matrix products, arithmetic and copies ran while one was open for 3% of the time, Pallas kernels for 0%

profile of v1, /device:TPU:0, one launch (start us, length us, event | category | flops | bytes accessed | tf_op | source)
XLA Modules:
  0.0 700.8 jit_solution(7238394680840896660)
XLA Ops:
  7.2 0.0 copy-start
  7.2 3.5 stack.2
  10.6 13.1 %all-to-all-start = ((bf16[64,16,2048]{2,1,0:T(8,128)(2,1)}), bf16[64,16,2048]{2,1,0:T(8,128)(2,1)}, u32[]{:S(2)}, u32[]{:S(2)}) async-start(bf16[64,16,2048]{2,1,0:T(8,128)(2,1)} %stack.2), calls=%async_computation | async-start | bytes 8388608 | tf_op jit(solution)/shard_map/all_to_all | solution.py:32
  23.7 0.0 all-gather.2.cloned.1.call-start
  23.8 0.7 all-gather.2.cloned.1.call-update
  24.5 0.0 all-reduce.3.cloned.1.call-start
  24.5 109.7 %all-to-all-done = bf16[64,16,2048]{2,1,0:T(8,128)(2,1)} async-done(((bf16[64,16,2048]{2,1,0:T(8,128)(2,1)}), bf16[64,16,2048]{2,1,0:T(8,128)(2,1)}, u32[]{:S(2)}, u32[]{:S(2)}) %all-to-all-start) | async-done | bytes 4194336 | tf_op jit(solution)/shard_map/all_to_all | solution.py:32
  134.2 6.2 fusion.5
  140.4 6.3 all-gather.2.cloned.1.call-done
  146.8 5.7 fusion.7
  152.4 3.3 fusion.6
  155.7 0.0 all-reduce.3.cloned.1.call-update
  155.8 0.2 reduce-scatter.2.cloned.1.call-start
  156.0 117.3 %all-reduce.3.cloned.1.call-done = (f32[1024,448]{0,1:T(8,128)}, f32[1024,448]{0,1:T(8,128)}, f32[1024,448]{0,1:T(8,128)}) async-done(((f32[1024,448]{0,1:T(8,128)}, f32[1024,448]{0,1:T(8,128)}, f32[1024,448]{0,1:T(8,128)}), (f32[1024,448]{0,1:T(8,128)}, f32[1024,448]{0,1:T(8,128)}, f32[1024,448]{0,1:T(8,128)})) %all-reduce.3.cloned.1.call-update) | async-done | bytes 5505040 | tf_op jit(solution)/shard_map/psum | solution.py:38
  273.3 3.7 multiply_convert_fusion.1
  277.0 2.4 fusion.8
  279.4 5.9 convolution_add_fusion
  285.3 0.0 reduce-scatter.2.cloned.1.call-update
  285.3 0.0 copy-start.6
  285.3 5.6 fusion.1
  291.0 3.3 fusion
  294.3 5.6 convolution_convert_fusion
  299.9 392.8 %reduce-scatter.2.cloned.1.call-done = f32[16,2048]{1,0:T(8,128)} async-done(((f32[1024,2048]{1,0:T(8,128)}), f32[16,2048]{1,0:T(8,128)}) %reduce-scatter.2.cloned.1.call-update) | async-done | bytes 131088 | tf_op jit(solution)/shard_map/reduce_scatter | solution.py:43
  692.7 1.5 convert_element_type.29
  (16 shorter events, 0.0 us)
Async XLA Ops:
  7.2 139.6 %copy-start = (bf16[2048,448]{0,1:T(8,128)(2,1)S(1)}, bf16[2048,448]{0,1:T(8,128)(2,1)}, u32[]{:S(2)}) copy-start(bf16[2048,448]{0,1:T(8,128)(2,1)} %param.7) | copy-start | bytes 5505028
  10.6 123.6 %all-to-all-start = ((bf16[64,16,2048]{2,1,0:T(8,128)(2,1)}), bf16[64,16,2048]{2,1,0:T(8,128)(2,1)}, u32[]{:S(2)}, u32[]{:S(2)}) async-start(bf16[64,16,2048]{2,1,0:T(8,128)(2,1)} %stack.2), calls=%async_computation | async-start | bytes 8388608 | tf_op jit(solution)/shard_map/all_to_all | solution.py:32
  23.7 123.0 %all-gather.2.cloned.1.call-start = ((), (), s32[]{:S(2)}) async-start(), calls=%async_computation.2 | async-start | bytes 4259840 | tf_op jit(solution)/shard_map/all_gather | solution.py:30
  24.5 248.8 %all-reduce.3.cloned.1.call-start = ((), (), s32[]{:S(2)}) async-start(), calls=%async_computation.4 | async-start | bytes 11010048 | tf_op jit(solution)/shard_map/psum | solution.py:38
  146.7 5.7 copy-start.1
  146.7 5.7 copy-start.7
  155.8 537.0 %reduce-scatter.2.cloned.1.call-start = ((), (), s32[]{:S(2)}) async-start(), calls=%async_computation.3 | async-start | bytes 8519680 | tf_op jit(solution)/shard_map/reduce_scatter | solution.py:43
  277.0 2.4 copy-start.5
  277.0 2.4 copy-start.2
  285.3 5.7 copy-start.6
  285.3 5.7 copy-start.8
  291.0 3.3 copy-start.3
  291.0 3.3 copy-start.4
Sparse Core Ops, SparseCore 0:
  27.9 118.8 all-gather.1
  155.9 117.3 all-reduce.2
  285.4 407.2 reduce-scatter.1
